TPU v7x, 256 devices: a whole 4x4x8 slice. The times are simulated.
256 devices in a mesh: seq: 32 (over x, z), head: 8 (over y, core).
Axes of the slice: x: 4, y: 4, z: 8, core: 2. Of those that a mesh axis runs over, the one named last changes fastest.
Arguments:
- tokens: bfloat16 [32768, 3072], P(('seq', 'head')), may hold values from -150 to 150
- norm_gain: float32 [3072], replicated, may hold values from 0.1 to 1.9
- w_query: bfloat16 [3072, 3072], P(None, 'head'), may hold values from -0.15625 to 0.15625
- w_key: bfloat16 [3072, 1024], P(None, 'head'), may hold values from -0.15625 to 0.15625
- w_value: bfloat16 [3072, 1024], P(None, 'head'), may hold values from -0.109375 to 0.109375
- w_out: bfloat16 [3072, 3072], P('head'), may hold values from -1.5 to 1.5
- long_cache: bfloat16 [2, 32768, 1024], P(None, 'seq', 'head'), may hold values from -244 to 244
- short_cache: bfloat16 [2, 8192, 1024], P(None, 'seq', 'head'), may hold values from -244 to 244
- slot_owner: int32 [8192], P('seq'), may hold values from -1 to 63, as said below
- new_len: int32 [64], replicated, may hold values from 2 to 1024, as said below
- cache_len: int32 [64], replicated, may hold values from 32 to 85, as said below
Outputs:
- layer_out: bfloat16 [32768, 3072], P(('seq', 'head'))
Inputs may be any that keep to these rules, and one draw needn't show every extreme that they name: `new_len`: lengths in order after the lead request's 64 tokens; they sum to 32704, and one request has exactly 1024 new tokens. `cache_len`: equals the number of short-cache slots that the request owns; one request has exactly 85. `slot_owner`: A request's slots are contiguous and lie in the block of 256 slots whose index equals that of the block of 1024 tokens holding the request's first new token.
All inputs are finite; a program needn't handle non-finite values.
Results may differ from a plain program's by a relative error of at most 0.02.
The roundings to bfloat16 on the way count: a program that leaves them out, or rounds other values in their place, can miss the bound.
Values may be sent and summed in bfloat16 or wider, within the bound.
A program may use at most 128 MiB of HBM per device.

v0:
```python
import math
import jax
import jax.numpy as jnp
from jax import lax
from jax.sharding import PartitionSpec as P

HD = 128
LEAD = 64
THETA_LOG = math.log(500000.0)


def from_behind(block, axis, distance):
    devices = range(lax.axis_size(axis))
    route = [(i - distance, i) for i in devices if i - distance in devices]
    return lax.ppermute(block, axis, route)


def rotate(field, position):
    half = field.shape[-1] // 2
    frequency = jnp.exp(jnp.arange(half, dtype=jnp.float32) * (-2.0 * THETA_LOG / field.shape[-1]))
    angle = position.astype(jnp.float32)[:, None] * frequency[None, :]
    cosine = jnp.cos(angle)[:, None, :]
    sine_part = jnp.sin(angle)[:, None, :]
    first_half = field[..., :half]
    second_half = field[..., half:]
    return jnp.concatenate(
        [
            first_half * cosine - second_half * sine_part,
            second_half * cosine + first_half * sine_part,
        ],
        axis=-1,
    )


def request_starts(new_len):
    return LEAD + jnp.cumsum(new_len) - new_len


def request_of(position_index, starts):
    passed = (starts[None, :] <= position_index[:, None]).astype(jnp.int32)
    request = jnp.sum(passed, axis=1) - 1
    return jnp.where(request < 0, starts.shape[0], request)


def position_of(position_index, request, starts, cache_len, long_len):
    number = starts.shape[0]
    select = jnp.arange(number, dtype=jnp.int32)[None, :] == request[:, None]
    begin = jnp.sum(jnp.where(select, starts[None, :], 0), axis=1)
    cached = jnp.sum(jnp.where(select, cache_len[None, :], 0), axis=1)
    return jnp.where(request == number, position_index + long_len, position_index - begin + cached)


def normalize(tokens, norm_gain):
    values = tokens.astype(jnp.float32)
    mean_square = jnp.mean(values * values, axis=-1, keepdims=True)
    return (values * lax.rsqrt(mean_square + 1e-05) * norm_gain).astype(jnp.bfloat16)


def raw_scores(queries, keys):
    return jnp.einsum("bgph,ngh->bgpn", queries, keys, preferred_element_type=jnp.float32) * (
        1.0 / math.sqrt(keys.shape[-1])
    )


def finish_state(scores, values):
    highest = jnp.max(scores, axis=-1)
    weights = jnp.exp(scores - highest[..., None])
    summed = jnp.sum(weights, axis=-1)
    mixture = jnp.einsum(
        "bgpn,ngh->bgph", weights.astype(jnp.bfloat16), values, preferred_element_type=jnp.float32
    )
    return (highest, summed, mixture)


def masked_state(queries, keys, values, valid):
    scores = jnp.where(valid[:, None, None, :], raw_scores(queries, keys), -jnp.inf)
    return finish_state(scores, values)


def plain_state(queries, keys, values):
    return finish_state(raw_scores(queries, keys), values)


def combine(former, latter):
    highest = jnp.maximum(former[0], latter[0])
    scale_former = jnp.exp(former[0] - highest)
    scale_latter = jnp.exp(latter[0] - highest)
    summed = former[1] * scale_former + latter[1] * scale_latter
    mixture = former[2] * scale_former[..., None] + latter[2] * scale_latter[..., None]
    return (highest, summed, mixture)


def on_device(
    tokens,
    norm_gain,
    w_query,
    w_key,
    w_value,
    w_out,
    long_cache,
    short_cache,
    slot_owner,
    new_len,
    cache_len,
):
    seq_index = lax.axis_index("seq")
    long_len = long_cache.shape[1] * lax.axis_size("seq")
    kv_heads = w_key.shape[1] // HD
    q_heads = w_query.shape[1] // HD
    per_kv = q_heads // kv_heads
    slots = short_cache.shape[1]
    q_width = w_query.shape[1]
    k_width = w_key.shape[1]
    earlier_slots, earlier_owner = from_behind((short_cache, slot_owner), "seq", 1)
    normed = normalize(tokens, norm_gain)
    piece = lax.all_gather(normed, "head", axis=0, tiled=True)
    projected = jnp.concatenate(
        [
            jnp.dot(piece, w_query, preferred_element_type=jnp.float32),
            jnp.dot(piece, w_key, preferred_element_type=jnp.float32),
            jnp.dot(piece, w_value, preferred_element_type=jnp.float32),
        ],
        axis=1,
    )
    local_rows = projected.shape[0]
    starts = request_starts(new_len)
    token_index = seq_index * local_rows + jnp.arange(local_rows, dtype=jnp.int32)
    request = request_of(token_index, starts)
    position = position_of(token_index, request, starts, cache_len, long_len)
    before_index = token_index - local_rows
    before_request = request_of(before_index, starts)
    queries = rotate(projected[:, :q_width].reshape(local_rows, q_heads, HD), position).astype(
        jnp.bfloat16
    )
    queries = queries.reshape(local_rows, kv_heads, per_kv, HD)
    keys = rotate(
        projected[:, q_width : q_width + k_width].reshape(local_rows, kv_heads, HD), position
    ).astype(jnp.bfloat16)
    values = projected[:, q_width + k_width :].astype(jnp.bfloat16)
    fresh = jnp.stack([keys.reshape(local_rows, k_width), values])
    earlier_fresh = from_behind(fresh, "seq", 1)
    has_before = seq_index > 0
    new_rows = jnp.concatenate([earlier_fresh, fresh], axis=1)
    new_keys = new_rows[0].reshape(-1, kv_heads, HD)
    new_values = new_rows[1].reshape(-1, kv_heads, HD)
    slot_rows = jnp.concatenate([earlier_slots, short_cache], axis=1)
    slot_keys = slot_rows[0].reshape(-1, kv_heads, HD)
    slot_values = slot_rows[1].reshape(-1, kv_heads, HD)
    new_request = jnp.concatenate([jnp.where(has_before, before_request, -1), request])
    new_index = jnp.concatenate([before_index, token_index])
    slot_request = jnp.concatenate([jnp.where(has_before, earlier_owner, -1), slot_owner]).astype(
        jnp.int32
    )
    slot_index = jnp.full((2 * slots,), -1, jnp.int32)
    block_rows = min(local_rows, 512)
    block_count = local_rows // block_rows
    window = local_rows + block_rows

    def local_block(item):
        block_queries, block_request, block_index, block_number = item
        begin = block_number * block_rows
        window_keys = jnp.concatenate(
            [lax.dynamic_slice_in_dim(new_keys, begin, window, 0), slot_keys], axis=0
        )
        window_values = jnp.concatenate(
            [lax.dynamic_slice_in_dim(new_values, begin, window, 0), slot_values], axis=0
        )
        window_request = jnp.concatenate(
            [lax.dynamic_slice_in_dim(new_request, begin, window, 0), slot_request]
        )
        window_index = jnp.concatenate(
            [lax.dynamic_slice_in_dim(new_index, begin, window, 0), slot_index]
        )
        valid = (window_request[None, :] == block_request[:, None]) & (
            window_index[None, :] <= block_index[:, None]
        )
        return masked_state(block_queries, window_keys, window_values, valid)

    highest, summed, mixture = lax.map(
        local_block,
        (
            queries.reshape(block_count, block_rows, kv_heads, per_kv, HD),
            request.reshape(block_count, block_rows),
            token_index.reshape(block_count, block_rows),
            jnp.arange(block_count, dtype=jnp.int32),
        ),
    )
    highest = highest.reshape(local_rows, kv_heads, per_kv)
    summed = summed.reshape(local_rows, kv_heads, per_kv)
    mixture = mixture.reshape(local_rows, kv_heads, per_kv, HD)
    lead_queries = queries[:LEAD]
    start_state = (
        jnp.full((LEAD, kv_heads, per_kv), -1e30, jnp.float32),
        jnp.zeros((LEAD, kv_heads, per_kv), jnp.float32),
        jnp.zeros((LEAD, kv_heads, per_kv, HD), jnp.float32),
    )
    piece = lax.all_gather(long_cache, "seq", axis=1, tiled=True)
    long_state = combine(
        start_state,
        plain_state(
            lead_queries, piece[0].reshape(-1, kv_heads, HD), piece[1].reshape(-1, kv_heads, HD)
        ),
    )
    long_highest = jnp.where(seq_index == 0, long_state[0], -1e30)
    joined = combine(
        (highest[:LEAD], summed[:LEAD], mixture[:LEAD]),
        (long_highest, long_state[1], long_state[2]),
    )
    summed = jnp.concatenate([joined[1], summed[LEAD:]], axis=0)
    mixture = jnp.concatenate([joined[2], mixture[LEAD:]], axis=0)
    attended = (mixture / summed[..., None]).astype(jnp.bfloat16).reshape(local_rows, q_width)
    gathered_sum = lax.psum_scatter(
        jnp.dot(attended, w_out, preferred_element_type=jnp.float32).astype(jnp.bfloat16),
        "head",
        scatter_dimension=0,
        tiled=True,
    )
    return gathered_sum


def solution(mesh):
    placed = (
        P(("seq", "head"), None),
        P(),
        P(None, "head"),
        P(None, "head"),
        P(None, "head"),
        P("head", None),
        P(None, "seq", "head"),
        P(None, "seq", "head"),
        P("seq"),
        P(),
        P(),
    )
    return jax.shard_map(
        on_device, mesh=mesh, in_specs=placed, out_specs=P(("seq", "head"), None), check_vma=False
    )
```

profile of v0, /device:TPU:1, one launch (start us, length us, event | category | flops | bytes accessed | tf_op | source)
XLA Modules:
  0.0 298.3 jit_solution(11702035966844528671)
XLA Ops:
  8.1 2.3 fusion.31
  11.2 4.4 %collective-permute-start = (s32[256]{0:T(256)}, s32[256]{0:T(256)S(1)}, u32[]{:S(2)}, u32[]{:S(2)}) collective-permute-start(s32[256]{0:T(256)} %param.21), channel_id=1, source_target_pairs={{0,8},{8,16},{16,24},{24,32},{32,40},{40,48},{48,56},{56,64},{64,7... | collective-permute-start | bytes 3080 | tf_op jit(solution)/shard_map/ppermute | solution.py:15
  15.6 3.6 %collective-permute-start.2 = (bf16[2,256,128]{2,1,0:T(8,128)(2,1)}, bf16[2,256,128]{2,1,0:T(8,128)(2,1)S(1)}, u32[]{:S(2)}, u32[]{:S(2)}) collective-permute-start(bf16[2,256,128]{2,1,0:T(8,128)(2,1)} %param.20), channel_id=1, source_target_pairs={{0,8},{8,16},{16,24},{24,32},{32,40},{40,48},{48,56},{56,64},{64,7... | collective-permute-start | bytes 393224 | tf_op jit(solution)/shard_map/ppermute | solution.py:15
  22.4 3.1 %multiply_cosine_fusion = (f32[1024,64]{1,0:T(8,128)}, f32[1024,64]{1,0:T(8,128)}) fusion(f32[64]{0:T(128)S(1)} %multiply_exponential_fusion, f32[1024]{0:T(1024)S(1)} %get-tuple-element.196), kind=kLoop, calls=%fused_computation.63 | loop fusion | flops 65536 | bytes 528640 | tf_op jit(solution)/shard_map/cos | solution.py:22
  28.1 30.1 %all-gather.3.cloned.1.call-done = bf16[1024,3072]{1,0:T(8,128)(2,1)} async-done(((bf16[128,3072]{1,0:T(8,128)(2,1)}), bf16[1024,3072]{1,0:T(8,128)(2,1)}) %all-gather.3.cloned.1.call-update) | async-done | bytes 6291472 | tf_op jit(solution)/shard_map/all_gather | solution.py:116
  58.3 5.3 %convolution_bitcast_fusion = f32[1024,1,128]{0,2,1:T(8,128)S(1)} fusion(bf16[1024,3072]{1,0:T(8,128)(2,1)} %all-gather.3.cloned.1.call-done, bf16[3072,128]{1,0:T(8,128)(2,1)} %param.16), kind=kOutput, calls=%fused_computation.51 | convolution fusion | flops 805306368 | bytes 7602176 | tf_op jit(solution)/shard_map/dot_general | solution.py:120
  64.8 2.2 fusion.33
  67.9 4.0 %collective-permute-start.1 = (bf16[2,1024,128]{1,2,0:T(8,128)(2,1)}, bf16[2,1024,128]{1,2,0:T(8,128)(2,1)}, u32[]{:S(2)}, u32[]{:S(2)}) collective-permute-start(bf16[2,1024,128]{1,2,0:T(8,128)(2,1)} %pad_maximum_fusion.1), channel_id=1, source_target_pairs={{0,8},{8,16},{16,24},{24,32},{32,40},{40,48},{48,56},{56,64},{64,7... | collective-permute-start | bytes 1572872 | tf_op jit(solution)/shard_map/ppermute | solution.py:15
  71.9 2.7 fusion.76
  75.6 2.8 copy.74
  80.0 2.6 subtract_convert_fusion
  84.9 4.6 %collective-permute-done.1 = bf16[2,1024,128]{1,2,0:T(8,128)(2,1)} collective-permute-done((bf16[2,1024,128]{1,2,0:T(8,128)(2,1)}, bf16[2,1024,128]{1,2,0:T(8,128)(2,1)}, u32[]{:S(2)}, u32[]{:S(2)}) %collective-permute-start.1) | collective-permute-done | bytes 524320 | tf_op jit(solution)/shard_map/ppermute | solution.py:15
  91.7 73.2 %while.14 = (s32[]{:T(128)}, f32[2,512,1,3]{1,0,3,2:T(2,128)}, f32[2,512,1,3]{1,0,2,3:T(2,128)}, f32[2,512,1,3,128]{4,1,0,3,2:T(8,128)}, s32[2]{0:T(128)S(1)}, /...) while((s32[]{:T(128)}, f32[2,512,1,3]{1,0,3,2:T(2,128)}, ...), condition=%wide.region_9.10_spmd, body=%wide.region_6.9_spmd.sunk | while | flops 1650459648 | bytes 50030996 | solution.py:179
  96.2 2.1 constant_dynamic-slice_fusion.7
  98.2 1.9 copy.86
  100.2 8.1 %fusion.90 = (f32[512,3]{0,1:T(4,128)S(1)}, f32[2048,512,3]{1,0,2:T(8,128)}) fusion(pred[512,2048]{0,1:T(8,128)(4,1)S(1)} %compare_and_fusion.2, bf16[2,512,1,3,128]{4,1,0,3,2:T(8,128)(2,1)} %get-tuple-element.368, s32[]{:T(128)S(6)} %copy.97, bf16[512,1,128]{2,0,1:T(8,128)(2,1)} %get-tuple-element.367, bf16[1536,1,128]{2,0,1:T(8,128)(2,1)} %copy.86), kind=kOutput, calls=%fused_computation.4.clone.1 | convolution fusion | flops 815790592 | bytes 14555140 | tf_op jit(solution)/shard_map/while/body/eval_jaxpr/bgph,ngh->bgpn/dot_general | solution.py:60
  108.4 7.3 %fusion.91 = f32[512,3]{0,1:T(4,128)S(1)} fusion(f32[2048,512,3]{1,0,2:T(8,128)} %get-tuple-element.311, f32[512,3]{0,1:T(4,128)S(1)} %get-tuple-element.310, pred[512,2048]{0,1:T(8,128)(4,1)S(1)} %compare_and_fusion.2), kind=kLoop, calls=%fused_computation.3.clone.1 | loop fusion | flops 12581376 | bytes 13643776 | tf_op jit(solution)/shard_map/while/body/eval_jaxpr/reduce_sum | solution.py:68
  115.8 10.4 %fusion.92 = f32[1,512,1,3,128]{1,4,3,2,0:T(8,128)} fusion(f32[2048,512,3]{1,0,2:T(8,128)} %get-tuple-element.311, f32[512,3]{0,1:T(4,128)S(1)} %get-tuple-element.310, pred[512,2048]{0,1:T(8,128)(4,1)S(1)} %compare_and_fusion.2, bf16[512,1,128]{0,2,1:T(8,128)(2,1)} %get-tuple-element.370, bf16[1536,1,128]{0,2,1:T(8,128)(2,1)} %get-tuple-element.312), kind=kOutput, calls=%fused_computation.9.clone.1 | convolution fusion | flops 818937856 | bytes 14948352 | tf_op jit(solution)/shard_map/while/body/eval_jaxpr/bgpn,ngh->bgph/dot_general | solution.py:69
  133.0 2.1 constant_dynamic-slice_fusion.7
  135.1 1.9 copy.86
  137.0 8.1 %fusion.90 = (f32[512,3]{0,1:T(4,128)S(1)}, f32[2048,512,3]{1,0,2:T(8,128)}) fusion(pred[512,2048]{0,1:T(8,128)(4,1)S(1)} %compare_and_fusion.2, bf16[2,512,1,3,128]{4,1,0,3,2:T(8,128)(2,1)} %get-tuple-element.368, s32[]{:T(128)S(6)} %copy.97, bf16[512,1,128]{2,0,1:T(8,128)(2,1)} %get-tuple-element.367, bf16[1536,1,128]{2,0,1:T(8,128)(2,1)} %copy.86), kind=kOutput, calls=%fused_computation.4.clone.1 | convolution fusion | flops 815790592 | bytes 14555140 | tf_op jit(solution)/shard_map/while/body/eval_jaxpr/bgph,ngh->bgpn/dot_general | solution.py:60
  145.2 7.6 %fusion.91 = f32[512,3]{0,1:T(4,128)S(1)} fusion(f32[2048,512,3]{1,0,2:T(8,128)} %get-tuple-element.311, f32[512,3]{0,1:T(4,128)S(1)} %get-tuple-element.310, pred[512,2048]{0,1:T(8,128)(4,1)S(1)} %compare_and_fusion.2), kind=kLoop, calls=%fused_computation.3.clone.1 | loop fusion | flops 12581376 | bytes 13643776 | tf_op jit(solution)/shard_map/while/body/eval_jaxpr/reduce_sum | solution.py:68
  152.9 9.6 %fusion.92 = f32[1,512,1,3,128]{1,4,3,2,0:T(8,128)} fusion(f32[2048,512,3]{1,0,2:T(8,128)} %get-tuple-element.311, f32[512,3]{0,1:T(4,128)S(1)} %get-tuple-element.310, pred[512,2048]{0,1:T(8,128)(4,1)S(1)} %compare_and_fusion.2, bf16[512,1,128]{0,2,1:T(8,128)(2,1)} %get-tuple-element.370, bf16[1536,1,128]{0,2,1:T(8,128)(2,1)} %get-tuple-element.312), kind=kOutput, calls=%fused_computation.9.clone.1 | convolution fusion | flops 818937856 | bytes 14948352 | tf_op jit(solution)/shard_map/while/body/eval_jaxpr/bgpn,ngh->bgph/dot_general | solution.py:69
  164.9 2.7 slice.77
  167.6 3.1 %copy.54 = f32[960,1,3,128]{0,3,2,1:T(8,128)} copy(f32[960,1,3,128]{3,0,2,1:T(8,128)} %slice.77) | data formatting | bytes 2949120 | tf_op jit(solution)/shard_map/slice | solution.py:210
  170.8 33.9 %all-gather.5.cloned.1.call-done = bf16[2,32768,128]{2,1,0:T(8,128)(2,1)} async-done(((bf16[2,1024,128]{2,1,0:T(8,128)(2,1)}), bf16[2,32768,128]{2,1,0:T(8,128)(2,1)}) %all-gather.5.cloned.1.call-update) | async-done | bytes 16777232 | tf_op jit(solution)/shard_map/all_gather | solution.py:197
  204.8 12.3 %fusion.75 = (f32[64,3]{0,1:T(4,128)S(1)}, f32[64,1,3,32768]{3,0,2,1:T(8,128)}) fusion(bf16[2,32768,128]{2,1,0:T(8,128)(2,1)} %all-gather.5.cloned.1.call-done, bf16[1024,3,64]{2,0,1:T(8,128)(2,1)} %copy-done.4, bf16[1024,3,64]{2,0,1:T(8,128)(2,1)S(1)} %copy-done.3), kind=kOutput, calls=%fused_computation.124 | convolution fusion | flops 1623293696 | bytes 34734848 | tf_op jit(solution)/shard_map/bgph,ngh->bgpn/dot_general | solution.py:60
  217.0 10.6 %fusion.23 = f32[64,3]{0,1:T(4,128)S(1)} fusion(f32[64,1,3,32768]{3,0,2,1:T(8,128)} %get-tuple-element.201, f32[64,3]{0,1:T(4,128)S(1)} %get-tuple-element.200), kind=kLoop, calls=%fused_computation.34 | loop fusion | flops 12582720 | bytes 25167360 | tf_op jit(solution)/shard_map/reduce_sum | solution.py:68
  227.7 14.4 %fusion.49 = f32[64,1,3,128]{3,0,2,1:T(8,128)S(1)} fusion(bf16[2,32768,128]{2,1,0:T(8,128)(2,1)} %all-gather.5.cloned.1.call-done, f32[64,1,3,32768]{3,0,2,1:T(8,128)} %get-tuple-element.201, f32[64,3]{0,1:T(4,128)S(1)} %get-tuple-element.200, f32[1024,1,3,128]{3,0,2,1:T(8,128)} %bitcast.189, f32[64,3]{0,1:T(4,128)S(1)} %bitcast.196, ...), kind=kOutput, calls=%fused_computation.59 | convolution fusion | flops 1623318528 | bytes 33754880 | tf_op jit(solution)/shard_map/bgpn,ngh->bgph/dot_general | solution.py:69
  242.4 1.9 fusion.32
  244.3 5.4 %convolution_convert_fusion = bf16[1024,3072]{1,0:T(8,128)(2,1)} fusion(bf16[1024,384]{0,1:T(8,128)(2,1)S(1)} %fusion.32, bf16[384,3072]{1,0:T(8,128)(2,1)S(1)} %copy-done), kind=kOutput, calls=%fused_computation.41 | convolution fusion | flops 2419064832 | bytes 9437184 | tf_op jit(solution)/shard_map/dot_general | solution.py:213
  249.7 42.1 %reduce-scatter.2.cloned.1.call-done = bf16[128,3072]{1,0:T(8,128)(2,1)} async-done(((bf16[1024,3072]{1,0:T(8,128)(2,1)}), bf16[128,3072]{1,0:T(8,128)(2,1)}) %reduce-scatter.2.cloned.1.call-update) | async-done | bytes 786448 | tf_op jit(solution)/shard_map/reduce_scatter | solution.py:212
  (118 shorter events, 30.3 us)
Async XLA Ops:
  6.5 237.7 %copy-start = (bf16[384,3072]{1,0:T(8,128)(2,1)S(1)}, bf16[384,3072]{1,0:T(8,128)(2,1)}, u32[]{:S(2)}) copy-start(bf16[384,3072]{1,0:T(8,128)(2,1)} %param.18) | copy-start | bytes 7077892
  6.5 20.1 %copy-start.8 = (bf16[2,256,128]{2,1,0:T(8,128)(2,1)S(1)}, bf16[2,256,128]{2,1,0:T(8,128)(2,1)}, u32[]{:S(2)}) copy-start(bf16[2,256,128]{2,1,0:T(8,128)(2,1)} %param.20) | copy-start | bytes 393220
  6.5 51.7 %all-gather.3.cloned.1.call-start = ((), (), s32[]{:S(2)}) async-start(), calls=%async_computation.1 | async-start | bytes 7077888 | tf_op jit(solution)/shard_map/all_gather | solution.py:116
  10.4 194.4 %all-gather.5.cloned.1.call-start = ((), (), s32[]{:S(2)}) async-start(), calls=%async_computation.2 | async-start | bytes 17301504 | tf_op jit(solution)/shard_map/all_gather | solution.py:197
  11.1 280.7 %reduce-scatter.2.cloned.1.call-start = ((), (), s32[]{:S(2)}) async-start(), calls=%async_computation.3 | async-start | bytes 7077888 | tf_op jit(solution)/shard_map/reduce_scatter | solution.py:212
  11.2 14.8 %collective-permute-start = (s32[256]{0:T(256)}, s32[256]{0:T(256)S(1)}, u32[]{:S(2)}, u32[]{:S(2)}) collective-permute-start(s32[256]{0:T(256)} %param.21), channel_id=1, source_target_pairs={{0,8},{8,16},{16,24},{24,32},{32,40},{40,48},{48,56},{56,64},{64,7... | collective-permute-start | bytes 3080 | tf_op jit(solution)/shard_map/ppermute | solution.py:15
  15.6 11.1 %collective-permute-start.2 = (bf16[2,256,128]{2,1,0:T(8,128)(2,1)}, bf16[2,256,128]{2,1,0:T(8,128)(2,1)S(1)}, u32[]{:S(2)}, u32[]{:S(2)}) collective-permute-start(bf16[2,256,128]{2,1,0:T(8,128)(2,1)} %param.20), channel_id=1, source_target_pairs={{0,8},{8,16},{16,24},{24,32},{32,40},{40,48},{48,56},{56,64},{64,7... | collective-permute-start | bytes 393224 | tf_op jit(solution)/shard_map/ppermute | solution.py:15
  28.1 36.6 %copy-start.7 = (bf16[3072,128]{1,0:T(8,128)(2,1)S(1)}, bf16[3072,128]{1,0:T(8,128)(2,1)}, u32[]{:S(2)}) copy-start(bf16[3072,128]{1,0:T(8,128)(2,1)} %param.17) | copy-start | bytes 2359300
  58.3 6.5 %copy-start.1 = (bf16[1024,3072]{1,0:T(8,128)(2,1)S(1)}, bf16[1024,3072]{1,0:T(8,128)(2,1)}, u32[]{:S(2)}) copy-start(bf16[1024,3072]{1,0:T(8,128)(2,1)} %all-gather.3.cloned.1.call-done) | copy-start | bytes 18874372
  64.8 2.2 copy-start.5
  64.8 7.1 %copy-start.15 = (bf16[3072,384]{1,0:T(8,128)(2,1)S(1)}, bf16[3072,384]{1,0:T(8,128)(2,1)}, u32[]{:S(2)}) copy-start(bf16[3072,384]{1,0:T(8,128)(2,1)} %param.15) | copy-start | bytes 7077892
  67.9 21.6 %collective-permute-start.1 = (bf16[2,1024,128]{1,2,0:T(8,128)(2,1)}, bf16[2,1024,128]{1,2,0:T(8,128)(2,1)}, u32[]{:S(2)}, u32[]{:S(2)}) collective-permute-start(bf16[2,1024,128]{1,2,0:T(8,128)(2,1)} %pad_maximum_fusion.1), channel_id=1, source_target_pairs={{0,8},{8,16},{16,24},{24,32},{32,40},{40,48},{48,56},{56,64},{64,7... | collective-permute-start | bytes 1572872 | tf_op jit(solution)/shard_map/ppermute | solution.py:15
  80.0 9.5 %copy-start.6 = (bf16[1,1024,64]{1,2,0:T(8,128)(2,1)S(1)}, bf16[1,1024,64]{1,2,0:T(8,128)(2,1)}, u32[]{:S(2)}) copy-start(bf16[1,1024,64]{1,2,0:T(8,128)(2,1)} %copy-done.5) | copy-start | bytes 393220
  82.6 0.9 copy-start.2
  82.6 2.2 copy-start.4
  100.2 8.1 %copy-start.9 = (f32[2,512,1,3]{1,0,3,2:T(2,128)S(1)}, f32[2,512,1,3]{1,0,3,2:T(2,128)}, u32[]{:S(2)}) copy-start(f32[2,512,1,3]{1,0,3,2:T(2,128)} %get-tuple-element.335) | copy-start | bytes 36868 | tf_op jit(solution)/shard_map/while
  108.4 7.3 %copy-start.10 = (f32[2,512,1,3]{1,0,3,2:T(2,128)}, f32[2,512,1,3]{1,0,3,2:T(2,128)S(1)}, u32[]{:S(2)}) copy-start(f32[2,512,1,3]{1,0,3,2:T(2,128)S(1)} %dynamic_update_slice.16) | copy-start | bytes 36868 | tf_op jit(solution)/shard_map/while
  108.4 7.3 %copy-start.12 = (f32[2,512,1,3]{1,0,2,3:T(2,128)S(1)}, f32[2,512,1,3]{1,0,2,3:T(2,128)}, u32[]{:S(2)}) copy-start(f32[2,512,1,3]{1,0,2,3:T(2,128)} %get-tuple-element.336) | copy-start | bytes 36868 | tf_op jit(solution)/shard_map/while
  115.8 10.4 %copy-start.13 = (f32[2,512,1,3]{1,0,2,3:T(2,128)}, f32[2,512,1,3]{1,0,2,3:T(2,128)S(1)}, u32[]{:S(2)}) copy-start(f32[2,512,1,3]{1,0,2,3:T(2,128)S(1)} %dynamic_update_slice.17) | copy-start | bytes 36868 | tf_op jit(solution)/shard_map/while
  137.0 8.1 %copy-start.9 = (f32[2,512,1,3]{1,0,3,2:T(2,128)S(1)}, f32[2,512,1,3]{1,0,3,2:T(2,128)}, u32[]{:S(2)}) copy-start(f32[2,512,1,3]{1,0,3,2:T(2,128)} %get-tuple-element.335) | copy-start | bytes 36868 | tf_op jit(solution)/shard_map/while
  145.2 7.6 %copy-start.10 = (f32[2,512,1,3]{1,0,3,2:T(2,128)}, f32[2,512,1,3]{1,0,3,2:T(2,128)S(1)}, u32[]{:S(2)}) copy-start(f32[2,512,1,3]{1,0,3,2:T(2,128)S(1)} %dynamic_update_slice.16) | copy-start | bytes 36868 | tf_op jit(solution)/shard_map/while
  145.2 7.6 %copy-start.12 = (f32[2,512,1,3]{1,0,2,3:T(2,128)S(1)}, f32[2,512,1,3]{1,0,2,3:T(2,128)}, u32[]{:S(2)}) copy-start(f32[2,512,1,3]{1,0,2,3:T(2,128)} %get-tuple-element.336) | copy-start | bytes 36868 | tf_op jit(solution)/shard_map/while
  152.9 9.6 %copy-start.13 = (f32[2,512,1,3]{1,0,2,3:T(2,128)}, f32[2,512,1,3]{1,0,2,3:T(2,128)S(1)}, u32[]{:S(2)}) copy-start(f32[2,512,1,3]{1,0,2,3:T(2,128)S(1)} %dynamic_update_slice.17) | copy-start | bytes 36868 | tf_op jit(solution)/shard_map/while
  164.9 5.8 %copy-start.14 = (f32[2,512,1,3]{1,0,2,3:T(2,128)S(1)}, f32[2,512,1,3]{1,0,2,3:T(2,128)}, u32[]{:S(2)}) copy-start(f32[2,512,1,3]{1,0,2,3:T(2,128)} %get-tuple-element.91) | copy-start | bytes 36868
  164.9 5.8 %copy-start.11 = (f32[2,512,1,3]{1,0,3,2:T(2,128)S(1)}, f32[2,512,1,3]{1,0,3,2:T(2,128)}, u32[]{:S(2)}) copy-start(f32[2,512,1,3]{1,0,3,2:T(2,128)} %get-tuple-element.90) | copy-start | bytes 36868
  164.9 39.9 %copy-start.3 = (bf16[1024,3,64]{2,0,1:T(8,128)(2,1)S(1)}, bf16[1024,3,64]{2,0,1:T(8,128)(2,1)}, u32[]{:S(2)}) copy-start(bf16[1024,3,64]{2,0,1:T(8,128)(2,1)} %copy-done.2) | copy-start | bytes 1179652
Sparse Core Ops, SparseCore 0:
  10.5 47.6 all-gather.2
  60.8 143.8 all-gather.4
  249.8 41.9 reduce-scatter.1
where the time goes:
time: 299 us; the launch traced here: 298 us
  waiting for transfers between devices  111 us (37%)
  matrix products  78.4 us (26%)
  other arithmetic  49.5 us (17%)
  local copies, waits for them, and re-layouts  31.9 us (11%)
  between operations  13.4 us (4%)
  starting transfers between devices  12 us (4%)
    reduce_scatter x1, waiting for transfers between devices, on_device(): lax.psum_scatter(jnp.dot(attended, w_out, preferred_element_type=jnp.floa...  42.1 us
    dot_general x3, matrix products, finish_state(): jnp.einsum('bgpn,ngh->bgph', weights.astype(jnp.bfloat16), values, prefer...  34.4 us
    all_gather x1, waiting for transfers between devices, on_device(): piece = lax.all_gather(long_cache, 'seq', axis=1, tiled=True)  33.9 us
    all_gather x1, waiting for transfers between devices, on_device(): piece = lax.all_gather(normed, 'head', axis=0, tiled=True)  30.1 us
    dot_general x3, matrix products, raw_scores(): jnp.einsum('bgph,ngh->bgpn', queries, keys, preferred_element_type=jnp.fl...  28.4 us
    reduce_sum x3, other arithmetic, finish_state(): summed = jnp.sum(weights, axis=-1)  25.5 us
    ppermute x3, starting transfers between devices, from_behind(): return lax.ppermute(block, axis, route)  11.9 us
  transfers between devices with their start and end apart: 6, of which 4 were waited for; matrix products, arithmetic and copies ran while one was open for 37% of the time, Pallas kernels for 0%

commit v1 on v0

--- a/solution.py
+++ b/solution.py
@@ -113,7 +113,14 @@
     k_width = w_key.shape[1]
     earlier_slots, earlier_owner = from_behind((short_cache, slot_owner), "seq", 1)
     normed = normalize(tokens, norm_gain)
-    piece = lax.all_gather(normed, "head", axis=0, tiled=True)
+    full_n = lax.axis_size("head")
+    tray = [normed]
+    for idx in range(full_n - 1):
+        tray.append(
+            lax.ppermute(tray[-1], "head", [(dev, (dev + 1) % full_n) for dev in range(full_n)])
+        )
+    tall = jnp.concatenate(tray[::-1], axis=0)
+    piece = jnp.roll(tall, shift=(lax.axis_index("head") + 1) * normed.shape[0], axis=0)
     projected = jnp.concatenate(
         [
             jnp.dot(piece, w_query, preferred_element_type=jnp.float32),

time: 299 us -> 325 us (1.087)
  starting transfers between devices: 12 us -> 28.5 us
  local copies, waits for them, and re-layouts: 31.9 us -> 47.5 us
  matrix products: 78.4 us -> 74.3 us
  other arithmetic: 49.5 us -> 45.7 us
    ppermute x0 -> x7, waiting for transfers between devices: none -> 49.2 us  [on_device(): lax.ppermute(tray[-1], 'head', [(dev, (dev + 1) % full_n) for dev in rang...]
    all_gather x1, waiting for transfers between devices: 33.9 us -> 0.02 us  [on_device(): piece = lax.all_gather(long_cache, 'seq', axis=1, tiled=True)]
    all_gather x1 -> x0, waiting for transfers between devices: 30.1 us -> none  [on_device(): piece = lax.all_gather(normed, 'head', axis=0, tiled=True)]
    ppermute x0 -> x7, starting transfers between devices: none -> 17.7 us  [on_device(): lax.ppermute(tray[-1], 'head', [(dev, (dev + 1) % full_n) for dev in rang...]
    unnamed x30 -> x48, local copies, waits for them, and re-layouts: 5.37 us -> 21.8 us
    reduce_scatter x1, waiting for transfers between devices: 42.1 us -> 56.6 us  [on_device(): lax.psum_scatter(jnp.dot(attended, w_out, preferred_element_type=jnp.floa...]
  transfers between devices with their start and end apart: 6 -> 12, of which waited for: 4 -> 9; matrix products, arithmetic and copies ran while one was open for 37% -> 37% of each run, Pallas kernels for 0% -> 0%
where the time goes in v1:
time: 325 us; the launch traced here: 324 us
  waiting for transfers between devices  113 us (35%)
  matrix products  74.3 us (23%)
  local copies, waits for them, and re-layouts  47.5 us (15%)
  other arithmetic  45.7 us (14%)
  starting transfers between devices  28.5 us (9%)
  between operations  13.8 us (4%)
    reduce_scatter x1, waiting for transfers between devices, on_device(): lax.psum_scatter(jnp.dot(attended, w_out, preferred_element_type=jnp.floa...  56.6 us
    ppermute x7, waiting for transfers between devices, on_device(): lax.ppermute(tray[-1], 'head', [(dev, (dev + 1) % full_n) for dev in rang...  49.2 us
    dot_general x3, matrix products, finish_state(): jnp.einsum('bgpn,ngh->bgph', weights.astype(jnp.bfloat16), values, prefer...  33 us
    dot_general x3, matrix products, raw_scores(): jnp.einsum('bgph,ngh->bgpn', queries, keys, preferred_element_type=jnp.fl...  28.6 us
    reduce_sum x3, other arithmetic, finish_state(): summed = jnp.sum(weights, axis=-1)  25.2 us
    unnamed x48, local copies, waits for them, and re-layouts  21.8 us
    ppermute x7, starting transfers between devices, on_device(): lax.ppermute(tray[-1], 'head', [(dev, (dev + 1) % full_n) for dev in rang...  17.7 us
    ppermute x3, starting transfers between devices, from_behind(): return lax.ppermute(block, axis, route)  10.7 us
  transfers between devices with their start and end apart: 12, of which 9 were waited for; matrix products, arithmetic and copies ran while one was open for 37% of the time, Pallas kernels for 0%

profile of v1, /device:TPU:1, one launch (start us, length us, event | category | flops | bytes accessed | tf_op | source)
XLA Modules:
  0.0 323.8 jit_solution(10707929959841465008)
XLA Ops:
  10.1 2.7 collective-permute-start.1
  12.8 8.9 %collective-permute-done.1 = bf16[128,3072]{1,0:T(8,128)(2,1)S(1)} collective-permute-done((bf16[128,3072]{1,0:T(8,128)(2,1)S(1)}, bf16[128,3072]{1,0:T(8,128)(2,1)S(1)}, u32[]{:S(2)}, u32[]{:S(2)}) %collective-permute-start.1) | collective-permute-done | bytes 786464 | tf_op jit(solution)/shard_map/ppermute | solution.py:120
  22.6 2.5 collective-permute-start.2
  25.1 8.9 %collective-permute-done.2 = bf16[128,3072]{1,0:T(8,128)(2,1)S(1)} collective-permute-done((bf16[128,3072]{1,0:T(8,128)(2,1)S(1)}, bf16[128,3072]{1,0:T(8,128)(2,1)S(1)}, u32[]{:S(2)}, u32[]{:S(2)}) %collective-permute-start.2) | collective-permute-done | bytes 786464 | tf_op jit(solution)/shard_map/ppermute | solution.py:120
  34.9 2.5 collective-permute-start.3
  37.4 8.9 %collective-permute-done.3 = bf16[128,3072]{1,0:T(8,128)(2,1)} collective-permute-done((bf16[128,3072]{1,0:T(8,128)(2,1)S(1)}, bf16[128,3072]{1,0:T(8,128)(2,1)}, u32[]{:S(2)}, u32[]{:S(2)}) %collective-permute-start.3) | collective-permute-done | bytes 786464 | tf_op jit(solution)/shard_map/ppermute | solution.py:120
  46.4 2.6 collective-permute-start.4
  48.9 3.5 %collective-permute-start = (s32[256]{0:T(256)}, s32[256]{0:T(256)S(1)}, u32[]{:S(2)}, u32[]{:S(2)}) collective-permute-start(s32[256]{0:T(256)} %param.21), channel_id=1, source_target_pairs={{0,8},{8,16},{16,24},{24,32},{32,40},{40,48},{48,56},{56,64},{64,7... | collective-permute-start | bytes 3080 | tf_op jit(solution)/shard_map/ppermute | solution.py:15
  52.5 3.6 %collective-permute-start.9 = (bf16[2,256,128]{2,1,0:T(8,128)(2,1)}, bf16[2,256,128]{2,1,0:T(8,128)(2,1)S(1)}, u32[]{:S(2)}, u32[]{:S(2)}) collective-permute-start(bf16[2,256,128]{2,1,0:T(8,128)(2,1)} %param.20), channel_id=1, source_target_pairs={{0,8},{8,16},{16,24},{24,32},{32,40},{40,48},{48,56},{56,64},{64,7... | collective-permute-start | bytes 393224 | tf_op jit(solution)/shard_map/ppermute | solution.py:15
  61.6 8.4 %collective-permute-done.5 = bf16[128,3072]{1,0:T(8,128)(2,1)} collective-permute-done((bf16[128,3072]{1,0:T(8,128)(2,1)}, bf16[128,3072]{1,0:T(8,128)(2,1)}, u32[]{:S(2)}, u32[]{:S(2)}) %collective-permute-start.5) | collective-permute-done | bytes 786464 | tf_op jit(solution)/shard_map/ppermute | solution.py:120
  72.4 3.1 multiply_cosine_fusion
  75.5 6.1 %collective-permute-done.6 = bf16[128,3072]{1,0:T(8,128)(2,1)} collective-permute-done((bf16[128,3072]{1,0:T(8,128)(2,1)}, bf16[128,3072]{1,0:T(8,128)(2,1)}, u32[]{:S(2)}, u32[]{:S(2)}) %collective-permute-start.6) | collective-permute-done | bytes 786464 | tf_op jit(solution)/shard_map/ppermute | solution.py:120
  86.6 7.5 %collective-permute-done.7 = bf16[128,3072]{1,0:T(8,128)(2,1)} collective-permute-done((bf16[128,3072]{1,0:T(8,128)(2,1)}, bf16[128,3072]{1,0:T(8,128)(2,1)}, u32[]{:S(2)}, u32[]{:S(2)}) %collective-permute-start.7) | collective-permute-done | bytes 786464 | tf_op jit(solution)/shard_map/ppermute | solution.py:120
  115.9 3.7 %collective-permute-start.8 = (bf16[2,1024,128]{1,2,0:T(8,128)(2,1)}, bf16[2,1024,128]{1,2,0:T(8,128)(2,1)}, u32[]{:S(2)}, u32[]{:S(2)}) collective-permute-start(bf16[2,1024,128]{1,2,0:T(8,128)(2,1)} %pad_maximum_fusion.1), channel_id=1, source_target_pairs={{0,8},{8,16},{16,24},{24,32},{32,40},{40,48},{48,56},{56,64},{64,7... | collective-permute-start | bytes 1572872 | tf_op jit(solution)/shard_map/ppermute | solution.py:15
  119.5 2.7 fusion.29
  123.3 2.8 copy.74
  127.7 2.6 subtract_convert_fusion
  132.4 6.1 %collective-permute-done.8 = bf16[2,1024,128]{1,2,0:T(8,128)(2,1)} collective-permute-done((bf16[2,1024,128]{1,2,0:T(8,128)(2,1)}, bf16[2,1024,128]{1,2,0:T(8,128)(2,1)}, u32[]{:S(2)}, u32[]{:S(2)}) %collective-permute-start.8) | collective-permute-done | bytes 524320 | tf_op jit(solution)/shard_map/ppermute | solution.py:15
  140.9 68.4 %while.14 = (s32[]{:T(128)}, f32[2,512,1,3]{1,0,3,2:T(2,128)S(1)}, f32[2,512,1,3]{1,0,2,3:T(2,128)S(1)}, f32[2,512,1,3,128]{4,1,0,3,2:T(8,128)}, s32[2]{0:T(128)...) while((s32[]{:T(128)}, f32[2,512,1,3]{1,0,3,2:T(2,128)S(1)}, ...), condition=%wide.region_9.10_spmd, body=%wide.region_6.9_spmd.sunk | while | flops 1650459648 | bytes 49834276 | solution.py:186
  147.9 8.1 %fusion.103 = (f32[512,3]{0,1:T(4,128)S(1)}, f32[2048,512,3]{1,0,2:T(8,128)}) fusion(pred[512,2048]{0,1:T(8,128)(4,1)S(1)} %compare_and_fusion.2, bf16[2,512,1,3,128]{4,1,0,3,2:T(8,128)(2,1)} %get-tuple-element.368, s32[]{:T(128)S(6)} %copy.112, bf16[512,1,128]{2,0,1:T(8,128)(2,1)} %get-tuple-element.367, bf16[1536,1,128]{2,0,1:T(8,128)(2,1)} %copy.86), kind=kOutput, calls=%fused_computation.4.clone.1 | convolution fusion | flops 815790592 | bytes 14555140 | tf_op jit(solution)/shard_map/while/body/eval_jaxpr/bgph,ngh->bgpn/dot_general | solution.py:60
  156.1 7.3 %fusion.104 = f32[512,3]{0,1:T(4,128)S(1)} fusion(f32[2048,512,3]{1,0,2:T(8,128)} %get-tuple-element.311, f32[512,3]{0,1:T(4,128)S(1)} %get-tuple-element.310, pred[512,2048]{0,1:T(8,128)(4,1)S(1)} %compare_and_fusion.2), kind=kLoop, calls=%fused_computation.3.clone.1 | loop fusion | flops 12581376 | bytes 13643776 | tf_op jit(solution)/shard_map/while/body/eval_jaxpr/reduce_sum | solution.py:68
  163.4 9.3 %fusion.105 = f32[1,512,1,3,128]{1,4,3,2,0:T(8,128)} fusion(f32[2048,512,3]{1,0,2:T(8,128)} %get-tuple-element.311, f32[512,3]{0,1:T(4,128)S(1)} %get-tuple-element.310, pred[512,2048]{0,1:T(8,128)(4,1)S(1)} %compare_and_fusion.2, bf16[512,1,128]{0,2,1:T(8,128)(2,1)} %get-tuple-element.370, bf16[1536,1,128]{0,2,1:T(8,128)(2,1)} %get-tuple-element.312), kind=kOutput, calls=%fused_computation.9.clone.1 | convolution fusion | flops 818937856 | bytes 14948352 | tf_op jit(solution)/shard_map/while/body/eval_jaxpr/bgpn,ngh->bgph/dot_general | solution.py:69
  182.1 8.1 %fusion.103 = (f32[512,3]{0,1:T(4,128)S(1)}, f32[2048,512,3]{1,0,2:T(8,128)}) fusion(pred[512,2048]{0,1:T(8,128)(4,1)S(1)} %compare_and_fusion.2, bf16[2,512,1,3,128]{4,1,0,3,2:T(8,128)(2,1)} %get-tuple-element.368, s32[]{:T(128)S(6)} %copy.112, bf16[512,1,128]{2,0,1:T(8,128)(2,1)} %get-tuple-element.367, bf16[1536,1,128]{2,0,1:T(8,128)(2,1)} %copy.86), kind=kOutput, calls=%fused_computation.4.clone.1 | convolution fusion | flops 815790592 | bytes 14555140 | tf_op jit(solution)/shard_map/while/body/eval_jaxpr/bgph,ngh->bgpn/dot_general | solution.py:60
  190.3 7.3 %fusion.104 = f32[512,3]{0,1:T(4,128)S(1)} fusion(f32[2048,512,3]{1,0,2:T(8,128)} %get-tuple-element.311, f32[512,3]{0,1:T(4,128)S(1)} %get-tuple-element.310, pred[512,2048]{0,1:T(8,128)(4,1)S(1)} %compare_and_fusion.2), kind=kLoop, calls=%fused_computation.3.clone.1 | loop fusion | flops 12581376 | bytes 13643776 | tf_op jit(solution)/shard_map/while/body/eval_jaxpr/reduce_sum | solution.py:68
  197.6 9.3 %fusion.105 = f32[1,512,1,3,128]{1,4,3,2,0:T(8,128)} fusion(f32[2048,512,3]{1,0,2:T(8,128)} %get-tuple-element.311, f32[512,3]{0,1:T(4,128)S(1)} %get-tuple-element.310, pred[512,2048]{0,1:T(8,128)(4,1)S(1)} %compare_and_fusion.2, bf16[512,1,128]{0,2,1:T(8,128)(2,1)} %get-tuple-element.370, bf16[1536,1,128]{0,2,1:T(8,128)(2,1)} %get-tuple-element.312), kind=kOutput, calls=%fused_computation.9.clone.1 | convolution fusion | flops 818937856 | bytes 14948352 | tf_op jit(solution)/shard_map/while/body/eval_jaxpr/bgpn,ngh->bgph/dot_general | solution.py:69
  209.3 2.6 slice.77
  211.9 3.0 copy.54
  215.1 12.5 %fusion.92 = (f32[64,3]{0,1:T(4,128)S(1)}, f32[64,1,3,32768]{3,0,2,1:T(8,128)}) fusion(bf16[2,32768,128]{2,1,0:T(8,128)(2,1)} %all-gather.2.cloned.1.call-done, bf16[1024,3,64]{2,0,1:T(8,128)(2,1)} %copy-done.3, bf16[1024,3,64]{2,0,1:T(8,128)(2,1)} %copy-done.2), kind=kOutput, calls=%fused_computation.149 | convolution fusion | flops 1623293696 | bytes 35128064 | tf_op jit(solution)/shard_map/bgph,ngh->bgpn/dot_general | solution.py:60
  227.6 10.6 %fusion.23 = f32[64,3]{0,1:T(4,128)S(1)} fusion(f32[64,1,3,32768]{3,0,2,1:T(8,128)} %get-tuple-element.201, f32[64,3]{0,1:T(4,128)S(1)} %get-tuple-element.200), kind=kLoop, calls=%fused_computation.34 | loop fusion | flops 12582720 | bytes 25167360 | tf_op jit(solution)/shard_map/reduce_sum | solution.py:68
  238.2 14.4 %fusion.63 = f32[64,1,3,128]{3,0,2,1:T(8,128)S(1)} fusion(bf16[2,32768,128]{2,1,0:T(8,128)(2,1)} %all-gather.2.cloned.1.call-done, f32[64,1,3,32768]{3,0,2,1:T(8,128)} %get-tuple-element.201, f32[64,3]{0,1:T(4,128)S(1)} %get-tuple-element.200, f32[1024,1,3,128]{3,0,2,1:T(8,128)} %bitcast.186, f32[64,3]{0,1:T(4,128)S(1)} %bitcast.193, ...), kind=kOutput, calls=%fused_computation.65 | convolution fusion | flops 1623318528 | bytes 33754880 | tf_op jit(solution)/shard_map/bgpn,ngh->bgph/dot_general | solution.py:69
  254.8 5.5 %convolution_convert_fusion = bf16[1024,3072]{1,0:T(8,128)(2,1)} fusion(bf16[1024,384]{0,1:T(8,128)(2,1)S(1)} %fusion.38, bf16[384,3072]{1,0:T(8,128)(2,1)S(1)} %copy-done), kind=kOutput, calls=%fused_computation.41 | convolution fusion | flops 2419064832 | bytes 9437184 | tf_op jit(solution)/shard_map/dot_general | solution.py:220
  260.3 56.6 %reduce-scatter.2.cloned.1.call-done = bf16[128,3072]{1,0:T(8,128)(2,1)} async-done(((bf16[1024,3072]{1,0:T(8,128)(2,1)}), bf16[128,3072]{1,0:T(8,128)(2,1)}) %reduce-scatter.2.cloned.1.call-update) | async-done | bytes 786448 | tf_op jit(solution)/shard_map/reduce_scatter | solution.py:219
  (133 shorter events, 67.0 us)
Async XLA Ops:
  6.5 248.3 %copy-start = (bf16[384,3072]{1,0:T(8,128)(2,1)S(1)}, bf16[384,3072]{1,0:T(8,128)(2,1)}, u32[]{:S(2)}) copy-start(bf16[384,3072]{1,0:T(8,128)(2,1)} %param.18) | copy-start | bytes 7077892
  6.5 96.1 %copy-start.1 = (bf16[128,3072]{1,0:T(8,128)(2,1)S(1)}, bf16[128,3072]{1,0:T(8,128)(2,1)}, u32[]{:S(2)}) copy-start(bf16[128,3072]{1,0:T(8,128)(2,1)} %param.13) | copy-start | bytes 2359300
  6.5 96.1 %copy-start.9 = (f32[3072]{0:T(1024)S(1)}, f32[3072]{0:T(1024)}, u32[]{:S(2)}) copy-start(f32[3072]{0:T(1024)} %param.14) | copy-start | bytes 36868
  6.5 208.5 %all-gather.2.cloned.1.call-start = ((), (), s32[]{:S(2)}) async-start(), calls=%async_computation.1 | async-start | bytes 17301504 | tf_op jit(solution)/shard_map/all_gather | solution.py:204
  7.3 309.7 %reduce-scatter.2.cloned.1.call-start = ((), (), s32[]{:S(2)}) async-start(), calls=%async_computation.2 | async-start | bytes 7077888 | tf_op jit(solution)/shard_map/reduce_scatter | solution.py:219
  10.1 11.6 %collective-permute-start.1 = (bf16[128,3072]{1,0:T(8,128)(2,1)S(1)}, bf16[128,3072]{1,0:T(8,128)(2,1)S(1)}, u32[]{:S(2)}, u32[]{:S(2)}) collective-permute-start(bf16[128,3072]{1,0:T(8,128)(2,1)S(1)} %fusion.37), channel_id=1, source_target_pairs={{0,1},{1,2},{2,3},{3,4},{4,5},{5,6},{6,7},{7,0},{8,9},{9,10},{10,1... | collective-permute-start | bytes 2359304 | tf_op jit(solution)/shard_map/ppermute | solution.py:120
  21.8 0.9 copy-start.4
  22.6 11.4 %collective-permute-start.2 = (bf16[128,3072]{1,0:T(8,128)(2,1)S(1)}, bf16[128,3072]{1,0:T(8,128)(2,1)S(1)}, u32[]{:S(2)}, u32[]{:S(2)}) collective-permute-start(bf16[128,3072]{1,0:T(8,128)(2,1)S(1)} %collective-permute-done.1), channel_id=1, source_target_pairs={{0,1},{1,2},{2,3},{3,4},{4,5},{5,6},{6,7},{7,0},{8,9},{9,10},{10,1... | collective-permute-start | bytes 2359304 | tf_op jit(solution)/shard_map/ppermute | solution.py:120
  34.1 0.9 copy-start.6
  34.9 11.4 %collective-permute-start.3 = (bf16[128,3072]{1,0:T(8,128)(2,1)S(1)}, bf16[128,3072]{1,0:T(8,128)(2,1)}, u32[]{:S(2)}, u32[]{:S(2)}) collective-permute-start(bf16[128,3072]{1,0:T(8,128)(2,1)S(1)} %collective-permute-done.2), channel_id=1, source_target_pairs={{0,1},{1,2},{2,3},{3,4},{4,5},{5,6},{6,7},{7,0},{8,9},{9,10},{10,1... | collective-permute-start | bytes 2359304 | tf_op jit(solution)/shard_map/ppermute | solution.py:120
  46.4 11.8 %collective-permute-start.4 = (bf16[128,3072]{1,0:T(8,128)(2,1)}, bf16[128,3072]{1,0:T(8,128)(2,1)}, u32[]{:S(2)}, u32[]{:S(2)}) collective-permute-start(bf16[128,3072]{1,0:T(8,128)(2,1)} %collective-permute-done.3), channel_id=1, source_target_pairs={{0,1},{1,2},{2,3},{3,4},{4,5},{5,6},{6,7},{7,0},{8,9},{9,10},{10,1... | collective-permute-start | bytes 2359304 | tf_op jit(solution)/shard_map/ppermute | solution.py:120
  48.9 35.2 %collective-permute-start = (s32[256]{0:T(256)}, s32[256]{0:T(256)S(1)}, u32[]{:S(2)}, u32[]{:S(2)}) collective-permute-start(s32[256]{0:T(256)} %param.21), channel_id=1, source_target_pairs={{0,8},{8,16},{16,24},{24,32},{32,40},{40,48},{48,56},{56,64},{64,7... | collective-permute-start | bytes 3080 | tf_op jit(solution)/shard_map/ppermute | solution.py:15
  52.5 31.7 %collective-permute-start.9 = (bf16[2,256,128]{2,1,0:T(8,128)(2,1)}, bf16[2,256,128]{2,1,0:T(8,128)(2,1)S(1)}, u32[]{:S(2)}, u32[]{:S(2)}) collective-permute-start(bf16[2,256,128]{2,1,0:T(8,128)(2,1)} %param.20), channel_id=1, source_target_pairs={{0,8},{8,16},{16,24},{24,32},{32,40},{40,48},{48,56},{56,64},{64,7... | collective-permute-start | bytes 393224 | tf_op jit(solution)/shard_map/ppermute | solution.py:15
  58.2 11.7 %collective-permute-start.5 = (bf16[128,3072]{1,0:T(8,128)(2,1)}, bf16[128,3072]{1,0:T(8,128)(2,1)}, u32[]{:S(2)}, u32[]{:S(2)}) collective-permute-start(bf16[128,3072]{1,0:T(8,128)(2,1)} %collective-permute-done.4), channel_id=1, source_target_pairs={{0,1},{1,2},{2,3},{3,4},{4,5},{5,6},{6,7},{7,0},{8,9},{9,10},{10,1... | collective-permute-start | bytes 2359304 | tf_op jit(solution)/shard_map/ppermute | solution.py:120
  69.9 11.7 %collective-permute-start.6 = (bf16[128,3072]{1,0:T(8,128)(2,1)}, bf16[128,3072]{1,0:T(8,128)(2,1)}, u32[]{:S(2)}, u32[]{:S(2)}) collective-permute-start(bf16[128,3072]{1,0:T(8,128)(2,1)} %collective-permute-done.5), channel_id=1, source_target_pairs={{0,1},{1,2},{2,3},{3,4},{4,5},{5,6},{6,7},{7,0},{8,9},{9,10},{10,1... | collective-permute-start | bytes 2359304 | tf_op jit(solution)/shard_map/ppermute | solution.py:120
  81.7 12.4 %collective-permute-start.7 = (bf16[128,3072]{1,0:T(8,128)(2,1)}, bf16[128,3072]{1,0:T(8,128)(2,1)}, u32[]{:S(2)}, u32[]{:S(2)}) collective-permute-start(bf16[128,3072]{1,0:T(8,128)(2,1)} %collective-permute-done.6), channel_id=1, source_target_pairs={{0,1},{1,2},{2,3},{3,4},{4,5},{5,6},{6,7},{7,0},{8,9},{9,10},{10,1... | collective-permute-start | bytes 2359304 | tf_op jit(solution)/shard_map/ppermute | solution.py:120
  86.6 22.4 %copy-start.7 = (bf16[128,3072]{1,0:T(8,128)(2,1)S(1)}, bf16[128,3072]{1,0:T(8,128)(2,1)}, u32[]{:S(2)}) copy-start(bf16[128,3072]{1,0:T(8,128)(2,1)} %copy-done.6) | copy-start | bytes 2359300
  86.6 22.5 %copy-start.5 = (bf16[128,3072]{1,0:T(8,128)(2,1)S(1)}, bf16[128,3072]{1,0:T(8,128)(2,1)}, u32[]{:S(2)}) copy-start(bf16[128,3072]{1,0:T(8,128)(2,1)} %copy-done.4) | copy-start | bytes 2359300
  86.6 22.8 %copy-start.12 = (bf16[3072,128]{1,0:T(8,128)(2,1)S(1)}, bf16[3072,128]{1,0:T(8,128)(2,1)}, u32[]{:S(2)}) copy-start(bf16[3072,128]{1,0:T(8,128)(2,1)} %param.16) | copy-start | bytes 2359300
  101.4 11.4 %copy-start.13 = (bf16[3072,128]{1,0:T(8,128)(2,1)S(1)}, bf16[3072,128]{1,0:T(8,128)(2,1)}, u32[]{:S(2)}) copy-start(bf16[3072,128]{1,0:T(8,128)(2,1)} %param.17) | copy-start | bytes 2359300
  109.0 10.6 %copy-start.11 = (bf16[3072,384]{1,0:T(8,128)(2,1)S(1)}, bf16[3072,384]{1,0:T(8,128)(2,1)}, u32[]{:S(2)}) copy-start(bf16[3072,384]{1,0:T(8,128)(2,1)} %param.15) | copy-start | bytes 7077892
  115.0 0.9 copy-start.8
  115.9 22.7 %collective-permute-start.8 = (bf16[2,1024,128]{1,2,0:T(8,128)(2,1)}, bf16[2,1024,128]{1,2,0:T(8,128)(2,1)}, u32[]{:S(2)}, u32[]{:S(2)}) collective-permute-start(bf16[2,1024,128]{1,2,0:T(8,128)(2,1)} %pad_maximum_fusion.1), channel_id=1, source_target_pairs={{0,8},{8,16},{16,24},{24,32},{32,40},{40,48},{48,56},{56,64},{64,7... | collective-permute-start | bytes 1572872 | tf_op jit(solution)/shard_map/ppermute | solution.py:15
  122.2 18.7 %copy-start.10 = (s32[256]{0:T(256)S(1)}, s32[256]{0:T(256)}, u32[]{:S(2)}) copy-start(s32[256]{0:T(256)} %param.21) | copy-start | bytes 3076
  130.2 0.9 copy-start.2
  130.2 2.2 copy-start.3
Sparse Core Ops, SparseCore 0:
  10.0 154.8 all-gather.1
  260.4 56.4 reduce-scatter.1
